TPU v7x, 1024 devices: a whole 4x8x16 slice. The times are simulated.
1024 devices in a mesh: grp: 32 (over x, y_hi, core), blk: 16 (over z), sub: 2 (over y_lo).
Axes of the slice: x: 4, y: 8 (y_hi: 4, y_lo: 2; y = y_hi * 2 + y_lo), z: 16, core: 2. Of those that a mesh axis runs over, the one named last changes fastest.
Arguments:
- clips: bfloat16 [16384, 128, 512], P(('grp', 'blk', 'sub')), may hold values from -6 to 6
- lengths: int32 [16384], P(('grp', 'blk', 'sub')), may hold values from 32 to 128, as said below
- assign: int32 [512, 32], P(('grp', 'blk'), 'sub'), may hold values from 0 to 31, each once within a row
- text: bfloat16 [16384, 1024], P(('grp', 'blk', 'sub')), may hold values from -6 to 6
- positives: int32 [32, 512], P('grp', ('blk', 'sub')), may hold values from 0 to 511, each once within a row
- conv_w: bfloat16 [1536, 512], replicated, may hold values from -0.15625 to 0.15625
- proj_w: bfloat16 [512, 1024], replicated, may hold values from -0.25 to 0.25
- logit_scale: float32 [], replicated, may hold values from 4 to 12
- logit_bias: float32 [], replicated, may hold values from -3 to -1
Outputs:
- audio_grad: float32 [16384, 1024], P(('grp', 'blk', 'sub'))
- text_grad: float32 [16384, 1024], P(('grp', 'blk', 'sub'))
Inputs may be any that keep to these rules, and one draw needn't show every extreme that they name: `lengths`: frames at or beyond a clip's length are padding; some clip has 128 frames. `assign`: each row lists each of its pair's 2 * 16 clips once; the first device of the pair takes the first 16 entries. `positives`: each row is a permutation: every text of a group is the match of exactly one audio slot of that group.
All inputs are finite; a program needn't handle non-finite values.
Results may differ from a plain program's by a relative error of at most 0.0045.
Values may be sent and summed in bfloat16 or wider, within the bound.
A program may use at most 32 MiB of HBM per device.

v0:
```python
import jax
import jax.numpy as jnp
from jax import lax
from jax.sharding import PartitionSpec as P


def laid_out(blocks, dim):
    blocks = jnp.moveaxis(blocks, 0, dim)
    shape = blocks.shape
    return blocks.reshape(*shape[:dim], shape[dim] * shape[dim + 1], *shape[dim + 2 :])


def from_everyone(array, axis):
    copies = jnp.broadcast_to(array, (lax.axis_size(axis), *array.shape))
    return lax.all_to_all(copies, axis, split_axis=0, concat_axis=0, tiled=True)


def gathered_copies(array, axis, dim):
    return laid_out(from_everyone(array, axis), dim)


def gather_axes(array, axes, dim):
    out = array
    for number in range(len(axes) - 1, -1, -1):
        out = lax.all_gather(out, axes[number], axis=dim, tiled=True)
    return out


def passed_along(block, axis, distance):
    devices = range(lax.axis_size(axis))
    route = [((i - distance) % len(devices), i) for i in devices]
    return lax.ppermute(block, axis, route)


def tower(clips, lengths, conv_w, proj_w):
    count_frames = clips.shape[1]
    half = count_frames // 2
    frame_ids = jnp.arange(count_frames, dtype=jnp.int32)
    inside = (frame_ids[None, :] < lengths[:, None])[:, :, None]
    kept = jnp.where(inside, clips, jnp.zeros((), clips.dtype))
    padded = jnp.pad(kept, ((0, 0), (1, 0), (0, 0)))
    stacked = jnp.concatenate(
        [
            padded[:, 0:count_frames:2],
            padded[:, 1:count_frames:2],
            padded[:, 2 : count_frames + 1 : 2],
        ],
        axis=2,
    )
    hidden = jax.nn.gelu(
        jnp.dot(stacked.reshape(-1, stacked.shape[2]), conv_w, preferred_element_type=jnp.float32)
    )
    hidden = hidden.reshape(clips.shape[0], half, -1)
    out_ids = jnp.arange(half, dtype=jnp.int32)
    valid = (2 * out_ids[None, :] < lengths[:, None])[:, :, None]
    counts = ((lengths + 1) // 2).astype(jnp.float32)
    pooled = (
        jnp.sum(jnp.where(valid, hidden, jnp.zeros((), hidden.dtype)), axis=1) / counts[:, None]
    ).astype(jnp.bfloat16)
    projected = jnp.dot(pooled, proj_w, preferred_element_type=jnp.float32)
    return (
        projected * lax.rsqrt(jnp.sum(projected * projected, axis=1, keepdims=True) + 1e-06)
    ).astype(jnp.bfloat16)


def normalize(values):
    wide = values.astype(jnp.float32)
    return (wide * lax.rsqrt(jnp.sum(wide * wide, axis=1, keepdims=True) + 1e-06)).astype(
        jnp.bfloat16
    )


def left_product(weights, block):
    return lax.dot_general(
        weights, block, (((0,), (0,)), ((), ())), preferred_element_type=jnp.float32
    )


def on_device(clips, lengths, assign, text, positives, conv_w, proj_w, logit_scale, logit_bias):
    slots = assign[0]
    own_embed = tower(clips, lengths, conv_w, proj_w)
    audio = gathered_copies(own_embed, "sub", 0)[slots]
    own_text = normalize(text)
    group_text = gather_axes(own_text, ("blk", "sub"), 0)
    prev_text = passed_along(group_text, "grp", 1)
    group_rows = group_text.shape[0]
    own_logits = (
        logit_scale
        * lax.dot_general(
            audio, group_text, (((1,), (1,)), ((), ())), preferred_element_type=jnp.float32
        )
        + logit_bias
    )
    next_logits = (
        logit_scale
        * lax.dot_general(
            audio, prev_text, (((1,), (1,)), ((), ())), preferred_element_type=jnp.float32
        )
        + logit_bias
    )
    hit = jnp.arange(group_rows, dtype=jnp.int32)[None, :] == positives[0][:, None]
    own_weights = jnp.where(hit, -jax.nn.sigmoid(-own_logits), jax.nn.sigmoid(own_logits)).astype(
        jnp.bfloat16
    )
    next_weights = jax.nn.sigmoid(next_logits).astype(jnp.bfloat16)
    audio_grad = logit_scale * (
        jnp.dot(own_weights, group_text, preferred_element_type=jnp.float32)
        + jnp.dot(next_weights, prev_text, preferred_element_type=jnp.float32)
    )
    audio_all = gather_axes(audio, ("blk", "sub"), 0)
    first_cols, second_cols = (
        lax.all_to_all(own_weights, ("blk", "sub"), split_axis=1, concat_axis=0, tiled=True),
        lax.all_to_all(next_weights, ("blk", "sub"), split_axis=1, concat_axis=0, tiled=True),
    )
    own_part = logit_scale * left_product(first_cols, audio_all)
    next_part = logit_scale * left_product(second_cols, audio_all)
    text_grad = own_part + passed_along(next_part, "grp", -1)
    return (audio_grad, text_grad)


def solution(mesh):
    in_specs = (
        P(("grp", "blk", "sub"), None, None),
        P(("grp", "blk", "sub")),
        P(("grp", "blk"), "sub"),
        P(("grp", "blk", "sub"), None),
        P("grp", ("blk", "sub")),
        P(),
        P(),
        P(),
        P(),
    )
    out_specs = (P(("grp", "blk", "sub"), None), P(("grp", "blk", "sub"), None))
    return jax.shard_map(
        on_device, mesh=mesh, in_specs=in_specs, out_specs=out_specs, check_vma=False
    )
```

profile of v0, /device:TPU:1, one launch (start us, length us, event | category | flops | bytes accessed | tf_op | source)
XLA Modules:
  0.0 186.2 jit_solution(6407312076839668661)
XLA Ops:
  9.1 4.2 %all_gather.12 = bf16[32,1024]{1,0:T(8,128)(2,1)} all-gather(bf16[16,1024]{1,0:T(8,128)(2,1)S(1)} %fusion.17), channel_id=1, replica_groups=mesh['grp'=32,'blk'=16,'sub'=2] {'sub'}, dimensions={0}, use_global_device_ids=true | all-gather | bytes 98304 | tf_op jit(solution)/shard_map/all_gather | solution.py:25
  14.0 1.8 broadcast_select_fusion
  15.8 2.3 %pad.4 = bf16[16,129,512]{2,1,0:T(8,128)(2,1)} pad(bf16[16,128,512]{2,1,0:T(8,128)(2,1)S(1)} %broadcast_select_fusion, bf16[]{:T(256)} %constant.14.clone.1), padding=0_0x1_0x0_0 | pad | bytes 4210690 | tf_op jit(solution)/shard_map/jit(_pad)/pad | solution.py:41
  18.0 7.9 %slice.10 = bf16[16,64,512]{2,1,0:T(8,128)(2,1)S(1)} slice(bf16[16,129,512]{2,1,0:T(8,128)(2,1)} %pad.4), slice={[0:16:1], [1:128:2], [0:512:1]} | slice | bytes 2097152 | tf_op jit(solution)/shard_map/slice | solution.py:45
  26.0 9.7 %slice.11 = bf16[16,64,512]{2,1,0:T(8,128)(2,1)} slice(bf16[16,129,512]{2,1,0:T(8,128)(2,1)} %pad.4), slice={[0:16:1], [2:129:2], [0:512:1]} | slice | bytes 2097152 | tf_op jit(solution)/shard_map/slice | solution.py:46
  35.6 9.5 %slice.9 = bf16[16,64,512]{2,1,0:T(8,128)(2,1)} slice(bf16[16,129,512]{2,1,0:T(8,128)(2,1)} %pad.4), slice={[0:16:1], [0:128:2], [0:512:1]} | slice | bytes 2097152 | tf_op jit(solution)/shard_map/slice | solution.py:44
  45.3 1.7 pad_maximum_fusion
  47.0 2.3 %select_reduce_fusion = f32[16,512]{1,0:T(8,128)S(1)} fusion(pred[16,64]{1,0:T(8,128)(4,1)S(1)} %broadcast_compare_fusion, bf16[1024,1536]{1,0:T(8,128)(2,1)S(1)} %bitcast.38, bf16[1536,512]{1,0:T(8,128)(2,1)S(1)} %copy-done), kind=kOutput, calls=%fused_computation.10 | convolution fusion | flops 1615847424 | bytes 4752384 | tf_op jit(solution)/shard_map/dot_general | solution.py:51
  50.5 3.3 %all-to-all-start = ((bf16[2,16,1024]{2,1,0:T(8,128)(2,1)}), bf16[2,16,1024]{2,1,0:T(8,128)(2,1)S(1)}, u32[]{:S(2)}, u32[]{:S(2)}) async-start(bf16[2,16,1024]{2,1,0:T(8,128)(2,1)} %broadcast_in_dim.42), calls=%async_computation | async-start | bytes 131072 | tf_op jit(solution)/shard_map/all_to_all | solution.py:15
  53.9 2.9 %all-to-all-done = bf16[2,16,1024]{2,1,0:T(8,128)(2,1)S(1)} async-done(((bf16[2,16,1024]{2,1,0:T(8,128)(2,1)}), bf16[2,16,1024]{2,1,0:T(8,128)(2,1)S(1)}, u32[]{:S(2)}, u32[]{:S(2)}) %all-to-all-start) | async-done | bytes 65568 | tf_op jit(solution)/shard_map/all_to_all | solution.py:15
  57.4 3.5 %all-gather = bf16[32,1024]{1,0:T(8,128)(2,1)} all-gather(bf16[16,1024]{1,0:T(8,128)(2,1)S(1)} %gather_fusion), channel_id=2, replica_groups=mesh['grp'=32,'blk'=16,'sub'=2] {'sub'}, dimensions={0}, use_global_device_ids=true | all-gather | bytes 98304 | tf_op jit(solution)/shard_map/all_gather | solution.py:25
  60.9 25.3 %all-gather.5.cloned.1.call-done = bf16[512,1024]{1,0:T(8,128)(2,1)} async-done(((bf16[32,1024]{1,0:T(8,128)(2,1)}), bf16[512,1024]{1,0:T(8,128)(2,1)}) %all-gather.5.cloned.1.call-update) | async-done | bytes 1048592 | tf_op jit(solution)/shard_map/all_gather | solution.py:25
  86.3 15.4 %collective-permute-start = (bf16[512,1024]{1,0:T(8,128)(2,1)}, bf16[512,1024]{1,0:T(8,128)(2,1)}, u32[]{:S(2)}, u32[]{:S(2)}) collective-permute-start(bf16[512,1024]{1,0:T(8,128)(2,1)} %all-gather.5.cloned.1.call-done), channel_id=1, source_target_pairs={{992,0},{0,32},{32,64},{64,96},{96,128},{128,160},{160,192},{192,2... | collective-permute-start | bytes 3145736 | tf_op jit(solution)/shard_map/ppermute | solution.py:32
  103.0 1.6 select_convert_fusion
  105.6 8.8 %all-to-all-start.1 = ((bf16[32,2,128]{2,1,0:T(2,128)(2,1)}), bf16[32,2,128]{2,1,0:T(2,128)(2,1)S(1)}, u32[]{:S(2)}, u32[]{:S(2)}) async-start(bf16[32,2,128]{2,1,0:T(2,128)(2,1)} %reshape.128), calls=%async_computation.1 | async-start | bytes 32768 | tf_op jit(solution)/shard_map/all_to_all | solution.py:112
  114.4 6.3 %collective-permute-done = bf16[512,1024]{1,0:T(8,128)(2,1)} collective-permute-done((bf16[512,1024]{1,0:T(8,128)(2,1)}, bf16[512,1024]{1,0:T(8,128)(2,1)}, u32[]{:S(2)}, u32[]{:S(2)}) %collective-permute-start) | collective-permute-done | bytes 1048608 | tf_op jit(solution)/shard_map/ppermute | solution.py:32
  120.6 1.6 fusion.15
  123.2 3.2 %all-to-all-done.1 = bf16[32,2,128]{2,1,0:T(2,128)(2,1)S(1)} async-done(((bf16[32,2,128]{2,1,0:T(2,128)(2,1)}), bf16[32,2,128]{2,1,0:T(2,128)(2,1)S(1)}, u32[]{:S(2)}, u32[]{:S(2)}) %all-to-all-start.1) | async-done | bytes 16416 | tf_op jit(solution)/shard_map/all_to_all | solution.py:112
  126.4 10.0 %all-to-all-start.2 = ((bf16[32,2,128]{2,1,0:T(2,128)(2,1)}), bf16[32,2,128]{2,1,0:T(2,128)(2,1)S(1)}, u32[]{:S(2)}, u32[]{:S(2)}) async-start(bf16[32,2,128]{2,1,0:T(2,128)(2,1)} %reshape.126), calls=%async_computation.2 | async-start | bytes 32768 | tf_op jit(solution)/shard_map/all_to_all | solution.py:113
  136.8 11.8 %all-to-all-done.2 = bf16[32,2,128]{2,1,0:T(2,128)(2,1)S(1)} async-done(((bf16[32,2,128]{2,1,0:T(2,128)(2,1)}), bf16[32,2,128]{2,1,0:T(2,128)(2,1)S(1)}, u32[]{:S(2)}, u32[]{:S(2)}) %all-to-all-start.2) | async-done | bytes 16416 | tf_op jit(solution)/shard_map/all_to_all | solution.py:113
  148.7 12.1 %all-gather.7.cloned.1.call-done = bf16[512,1024]{1,0:T(8,128)(2,1)} async-done(((bf16[32,1024]{1,0:T(8,128)(2,1)}), bf16[512,1024]{1,0:T(8,128)(2,1)}) %all-gather.7.cloned.1.call-update) | async-done | bytes 1048592 | tf_op jit(solution)/shard_map/all_gather | solution.py:25
  160.8 1.6 convolution_multiply_fusion
  162.4 12.5 %collective-permute-start.1 = (f32[16,1024]{1,0:T(8,128)S(1)}, f32[16,1024]{1,0:T(8,128)S(1)}, u32[]{:S(2)}, u32[]{:S(2)}) collective-permute-start(f32[16,1024]{1,0:T(8,128)S(1)} %convolution_multiply_fusion), channel_id=1, source_target_pairs={{32,0},{64,32},{96,64},{128,96},{160,128},{192,160},{224,192},{256... | collective-permute-start | bytes 196616 | tf_op jit(solution)/shard_map/ppermute | solution.py:32
  174.9 2.1 %fusion.8 = f32[16,1024]{1,0:T(8,128)} fusion(f32[16,1024]{1,0:T(8,128)S(1)} %fusion.22, bf16[16,512]{1,0:T(8,128)(2,1)S(1)} %fusion.15, bf16[512,1024]{1,0:T(8,128)(2,1)} %collective-permute-done, f32[]{:T(128)S(6)} %copy.23), kind=kOutput, calls=%fused_computation.16 | convolution fusion | flops 16809984 | bytes 1196036 | tf_op jit(solution)/shard_map/dot_general | solution.py:108
  (43 shorter events, 9.3 us)
Async XLA Ops:
  7.2 39.8 %copy-start = (bf16[1536,512]{1,0:T(8,128)(2,1)S(1)}, bf16[1536,512]{1,0:T(8,128)(2,1)}, u32[]{:S(2)}) copy-start(bf16[1536,512]{1,0:T(8,128)(2,1)} %param.14) | copy-start | bytes 4718596
  7.2 79.1 %all-gather.5.cloned.1.call-start = ((), (), s32[]{:S(2)}) async-start(), calls=%async_computation.3 | async-start | bytes 1114112 | tf_op jit(solution)/shard_map/all_gather | solution.py:25
  26.0 19.2 %copy-start.4 = (s32[16]{0:T(128)S(1)}, s32[16]{0:T(128)}, u32[]{:S(2)}) copy-start(s32[16]{0:T(128)} %param.10) | copy-start | bytes 196
  47.0 2.4 %copy-start.3 = (bf16[512,1024]{1,0:T(8,128)(2,1)S(1)}, bf16[512,1024]{1,0:T(8,128)(2,1)}, u32[]{:S(2)}) copy-start(bf16[512,1024]{1,0:T(8,128)(2,1)} %param.15) | copy-start | bytes 3145732
  47.0 6.9 %copy-start.6 = (s32[1,16]{1,0:T(1,128)S(1)}, s32[1,16]{1,0:T(1,128)}, u32[]{:S(2)}) copy-start(s32[1,16]{1,0:T(1,128)} %param.11) | copy-start | bytes 196
  47.0 56.0 %copy-start.5 = (s32[1,16]{1,0:T(1,128)S(1)}, s32[1,16]{1,0:T(1,128)}, u32[]{:S(2)}) copy-start(s32[1,16]{1,0:T(1,128)} %param.13) | copy-start | bytes 196
  50.5 6.3 %all-to-all-start = ((bf16[2,16,1024]{2,1,0:T(8,128)(2,1)}), bf16[2,16,1024]{2,1,0:T(8,128)(2,1)S(1)}, u32[]{:S(2)}, u32[]{:S(2)}) async-start(bf16[2,16,1024]{2,1,0:T(8,128)(2,1)} %broadcast_in_dim.42), calls=%async_computation | async-start | bytes 131072 | tf_op jit(solution)/shard_map/all_to_all | solution.py:15
  53.8 107.0 %all-gather.7.cloned.1.call-start = ((), (), s32[]{:S(2)}) async-start(), calls=%async_computation.4 | async-start | bytes 1114112 | tf_op jit(solution)/shard_map/all_gather | solution.py:25
  86.3 50.1 %copy-start.1 = (bf16[512,1024]{1,0:T(8,128)(2,1)S(1)}, bf16[512,1024]{1,0:T(8,128)(2,1)}, u32[]{:S(2)}) copy-start(bf16[512,1024]{1,0:T(8,128)(2,1)} %all-gather.5.cloned.1.call-done) | copy-start | bytes 3145732
  86.3 34.4 %collective-permute-start = (bf16[512,1024]{1,0:T(8,128)(2,1)}, bf16[512,1024]{1,0:T(8,128)(2,1)}, u32[]{:S(2)}, u32[]{:S(2)}) collective-permute-start(bf16[512,1024]{1,0:T(8,128)(2,1)} %all-gather.5.cloned.1.call-done), channel_id=1, source_target_pairs={{992,0},{0,32},{32,64},{64,96},{96,128},{128,160},{160,192},{192,2... | collective-permute-start | bytes 3145736 | tf_op jit(solution)/shard_map/ppermute | solution.py:32
  105.6 20.8 %all-to-all-start.1 = ((bf16[32,2,128]{2,1,0:T(2,128)(2,1)}), bf16[32,2,128]{2,1,0:T(2,128)(2,1)S(1)}, u32[]{:S(2)}, u32[]{:S(2)}) async-start(bf16[32,2,128]{2,1,0:T(2,128)(2,1)} %reshape.128), calls=%async_computation.1 | async-start | bytes 32768 | tf_op jit(solution)/shard_map/all_to_all | solution.py:112
  126.4 22.2 %all-to-all-start.2 = ((bf16[32,2,128]{2,1,0:T(2,128)(2,1)}), bf16[32,2,128]{2,1,0:T(2,128)(2,1)S(1)}, u32[]{:S(2)}, u32[]{:S(2)}) async-start(bf16[32,2,128]{2,1,0:T(2,128)(2,1)} %reshape.126), calls=%async_computation.2 | async-start | bytes 32768 | tf_op jit(solution)/shard_map/all_to_all | solution.py:113
  160.8 17.7 %copy-start.2 = (bf16[512,1024]{1,0:T(8,128)(2,1)S(1)}, bf16[512,1024]{1,0:T(8,128)(2,1)}, u32[]{:S(2)}) copy-start(bf16[512,1024]{1,0:T(8,128)(2,1)} %all-gather.7.cloned.1.call-done) | copy-start | bytes 3145732
  162.4 16.1 %collective-permute-start.1 = (f32[16,1024]{1,0:T(8,128)S(1)}, f32[16,1024]{1,0:T(8,128)S(1)}, u32[]{:S(2)}, u32[]{:S(2)}) collective-permute-start(f32[16,1024]{1,0:T(8,128)S(1)} %convolution_multiply_fusion), channel_id=1, source_target_pairs={{32,0},{64,32},{96,64},{128,96},{160,128},{192,160},{224,192},{256... | collective-permute-start | bytes 196616 | tf_op jit(solution)/shard_map/ppermute | solution.py:32
Sparse Core Ops, SparseCore 0:
  13.4 72.8 all-gather.4
  88.9 71.8 all-gather.6
where the time goes:
time: 189 us; the launch traced here: 186 us
  waiting for transfers between devices  63 us (33%)
  starting transfers between devices  50.1 us (27%)
  local copies, waits for them, and re-layouts  32.8 us (17%)
  between operations  15.6 us (8%)
  matrix products  10.9 us (6%)
  blocking collectives  7.7 us (4%)
  other arithmetic  6.2 us (3%)
    all_gather x2, waiting for transfers between devices, gather_axes(): out = lax.all_gather(out, axes[number], axis=dim, tiled=True)  37.4 us
    ppermute x2, starting transfers between devices, passed_along(): return lax.ppermute(block, axis, route)  27.9 us
    all_to_all x1, waiting for transfers between devices, on_device(): lax.all_to_all(next_weights, ('blk', 'sub'), split_axis=1, concat_axis=0,...  11.8 us
    all_to_all x1, starting transfers between devices, on_device(): lax.all_to_all(next_weights, ('blk', 'sub'), split_axis=1, concat_axis=0,...  10 us
    slice x1, local copies, waits for them, and re-layouts, tower(): padded[:, 2:count_frames + 1:2]  9.67 us
    slice x1, local copies, waits for them, and re-layouts, tower(): padded[:, 0:count_frames:2]  9.52 us
    all_to_all x1, starting transfers between devices, on_device(): lax.all_to_all(own_weights, ('blk', 'sub'), split_axis=1, concat_axis=0,...  8.78 us
    slice x1, local copies, waits for them, and re-layouts, tower(): padded[:, 1:count_frames:2]  7.93 us
  transfers between devices with their start and end apart: 7, of which 7 were waited for; matrix products, arithmetic and copies ran while one was open for 24% of the time, Pallas kernels for 0%

commit v1 on v0

v1 whole, which is shorter than its diff:
```python
import functools
import math

import jax
import jax.numpy as jnp
from jax import lax
from jax.experimental import pallas as pl
from jax.experimental.pallas import tpu as pltpu
from jax.sharding import PartitionSpec as P

MESH = pl.DeviceIdType.MESH
ROWS = 16
FRAMES = 128
HALF = 64
CH = 512
E = 1024
EXT = 128
TEXT, AUDIO = 0, 1
TEXT_PARENT = {d: d - 1 for d in range(1, 17)}
AUDIO_PARENT = {d: d - 1 for d in range(1, 17)}
CHUNK = 4


def dot_nn(a, b):
    return jnp.dot(a, b, preferred_element_type=jnp.float32)


def dot_nt(a, b):
    return lax.dot_general(a, b, (((1,), (1,)), ((), ())), preferred_element_type=jnp.float32)


def gelu(x):
    inner = math.sqrt(2.0 / math.pi) * (x + 0.044715 * (x * x * x))
    return 0.5 * x * (1.0 + jnp.tanh(inner))


def unit_rows(wide):
    return wide * lax.rsqrt(jnp.sum(wide * wide, axis=1, keepdims=True) + 1e-06)


def weights_of(logits, hit):
    signed = jnp.where(hit, -logits, logits)
    s = jax.nn.sigmoid(signed)
    return jnp.where(hit, -s, s).astype(jnp.bfloat16)


def kernel(
    nz, ng,
    scale_ref, bias_ref, len_ref, assign_ref, pos_ref, text_hbm, clips_hbm, convw_hbm, projw_hbm,
    ag_ref, tg_ref,
    text_v, clips_v, convw_v, projw_v, picked, pool_f, zbuf, praw, pbuf, zx, px, own_a, own_t,
    back_a, got_a, back_t, got_t,
    load_sem, pair_send, pair_recv, ring_send, ring_recv, cross_send, cross_recv,
):
    g, z, s = lax.axis_index("grp"), lax.axis_index("blk"), lax.axis_index("sub")
    other = 1 - s
    up, down = lax.rem(g + 1, ng), lax.rem(g + ng - 1, ng)
    far = nz // 2
    parents = {TEXT: TEXT_PARENT, AUDIO: AUDIO_PARENT}
    bufs = {TEXT: zbuf, AUDIO: pbuf}
    scale, bias = scale_ref[0], bias_ref[0]

    def at_z(offset):
        return lax.rem(z + offset + 2 * nz, nz)

    n_chunks = ROWS // CHUNK
    loads = {"text": pltpu.make_async_copy(text_hbm, text_v, load_sem.at[0])}
    loads["conv"] = pltpu.make_async_copy(convw_hbm, convw_v, load_sem.at[1])
    loads["proj"] = pltpu.make_async_copy(projw_hbm, projw_v, load_sem.at[2])
    for i in range(n_chunks):
        part = pl.ds(i * CHUNK, CHUNK)
        loads[i] = pltpu.make_async_copy(clips_hbm.at[part], clips_v.at[part], load_sem.at[3 + i])
    for name in ("text", 0, "conv", *range(1, n_chunks), "proj"):
        loads[name].start()

    jumps = sorted({d - p for table in parents.values() for d, p in table.items() if d <= far})
    barrier = pltpu.get_barrier_semaphore()
    greeted = [{"sub": other}, {"grp": up}, {"grp": down}]
    for jump in jumps:
        greeted += [{"blk": at_z(jump)}, {"blk": at_z(-jump)}]
    for device in greeted:
        pl.semaphore_signal(barrier, inc=1, device_id=device, device_id_type=MESH)

    loads["text"].wait()
    zt = unit_rows(text_v[...].astype(jnp.float32)).astype(jnp.bfloat16)
    diagonal = lax.broadcasted_iota(jnp.int32, (ROWS, ROWS), 0) == lax.broadcasted_iota(
        jnp.int32, (ROWS, ROWS), 1
    )

    def column(row):
        return jnp.sum(jnp.where(diagonal, row, 0), axis=1, keepdims=True)

    pos_col = column(pos_ref[...])
    assign_col = column(assign_ref[...])
    lane = lax.broadcasted_iota(jnp.int32, (ROWS, EXT), 1)
    extra = jnp.where(lane == 0, pos_col >> 8, jnp.where(lane == 1, pos_col & 255, 0))
    extra = jnp.where(lane == 2, assign_col, extra)
    zbuf[z, s, :, pl.ds(0, E)] = zt
    zbuf[z, s, :, pl.ds(E, EXT)] = extra.astype(jnp.float32).astype(jnp.bfloat16)

    pl.semaphore_wait(barrier, len(greeted))

    sent = []

    def ring_copy(kind, sign, d, r):
        hop = d - parents[kind][d]
        here = bufs[kind].at[at_z(-sign * (d - hop)), s if r == 0 else other]
        return pltpu.make_async_remote_copy(
            src_ref=here, dst_ref=here,
            send_sem=ring_send.at[kind, (1 - sign) // 2, d - 1, r],
            recv_sem=ring_recv.at[kind, (1 - sign) // 2, d - 1, r],
            device_id={"blk": at_z(sign * hop)}, device_id_type=MESH,
        )

    def travels(sign, d, r):
        return d < far or (d == far and r == (1 - sign) // 2)

    def pass_on(kind, d, r, signs=(1, -1)):
        for child in range(far, d, -1):
            if parents[kind][child] == d:
                for sign in signs:
                    if travels(sign, child, r):
                        copy = ring_copy(kind, sign, child, r)
                        copy.start()
                        sent.append(copy)

    def arrived(kind, sign, d, r):
        landed = bufs[kind].at[at_z(-sign * d), s if r == 0 else other]
        pltpu.make_async_remote_copy(
            src_ref=landed, dst_ref=landed,
            send_sem=ring_send.at[kind, (1 - sign) // 2, d - 1, r],
            recv_sem=ring_recv.at[kind, (1 - sign) // 2, d - 1, r],
            device_id={"blk": at_z(sign)}, device_id_type=MESH,
        ).wait_recv()

    def relay(kind, d):
        for r in (0, 1):
            for sign in (1, -1):
                if travels(sign, d, r):
                    arrived(kind, sign, d, r)
                    pass_on(kind, d, r, (sign,))

    def remote(src, dst, send, recv, device):
        return pltpu.make_async_remote_copy(
            src_ref=src, dst_ref=dst, send_sem=send, recv_sem=recv, device_id=device,
            device_id_type=MESH,
        )

    def launch(copy):
        copy.start()
        sent.append(copy)
        return copy

    pass_on(TEXT, 0, 0)
    mine = zbuf.at[z, s]
    text_pair = launch(remote(mine, mine, pair_send.at[0], pair_recv.at[0], {"sub": other}))
    text_up = launch(remote(mine, zx, cross_send.at[0], cross_recv.at[0], {"grp": up}))

    frame = lax.broadcasted_iota(jnp.int32, (3 * HALF, FRAMES), 1)
    place = lax.broadcasted_iota(jnp.int32, (3 * HALF, FRAMES), 0)
    tap = (place >= HALF).astype(jnp.int32) + (place >= 2 * HALF).astype(jnp.int32)
    wanted = 2 * (place - HALF * tap) + tap - 1
    out_id = lax.broadcasted_iota(jnp.int32, (HALF, CH), 0)

    def tower_chunk(i):
        loads[i].wait()
        for c in range(CHUNK):
            clip = i * CHUNK + c
            length = len_ref[clip]
            choose = jnp.where((wanted == frame) & (frame < length), 1.0, 0.0).astype(jnp.bfloat16)
            rows = dot_nn(choose, clips_v[clip]).astype(jnp.bfloat16)
            for k in range(3):
                picked[pl.ds(c * HALF, HALF), pl.ds(k * CH, CH)] = rows[k * HALF : (k + 1) * HALF]
        if i == 0:
            loads["conv"].wait()
        hidden = gelu(dot_nn(picked[...], convw_v[...]))
        for c in range(CHUNK):
            clip = i * CHUNK + c
            length = len_ref[clip]
            kept = jnp.where(2 * out_id < length, hidden[c * HALF : (c + 1) * HALF], 0.0)
            total = jnp.sum(kept, axis=0, keepdims=True)
            count = jnp.full((1, CH), (length + 1) >> 1, jnp.int32).astype(jnp.float32)
            pool_f[pl.ds(clip, 1), :] = total / count

    def pair_texts():
        text_pair.wait_recv()
        pass_on(TEXT, 0, 1)

    tower_chunk(0)
    tower_chunk(1)
    pair_texts()
    tower_chunk(2)
    relay(TEXT, 1)
    tower_chunk(3)

    praw[s] = pool_f[...].astype(jnp.bfloat16)
    audio_pair = launch(
        remote(praw.at[s], praw.at[s], pair_send.at[1], pair_recv.at[1], {"sub": other})
    )
    relay(TEXT, 2)
    loads["proj"].wait()
    audio_pair.wait_recv()
    slot_clip = zbuf[z, :, :, pl.ds(E, EXT)].reshape(2 * ROWS, EXT).astype(jnp.float32)[:, 2:3]
    clip_id = lax.broadcasted_iota(jnp.int32, (2 * ROWS, 2 * ROWS), 1).astype(jnp.float32)
    order = jnp.where(slot_clip == clip_id, 1.0, 0.0).astype(jnp.bfloat16)
    slots = dot_nn(order, praw[...].reshape(2 * ROWS, CH)).astype(jnp.bfloat16)
    pbuf[z] = slots.reshape(2, ROWS, CH)
    pass_on(AUDIO, 0, 0)
    pass_on(AUDIO, 0, 1)
    mine_p = pbuf.at[z, s]
    audio_down = launch(remote(mine_p, px, cross_send.at[1], cross_recv.at[1], {"grp": down}))

    text_up.wait_recv()
    mine_first = lax.broadcasted_iota(jnp.int32, (2 * ROWS, 1), 0)
    own_texts = jnp.concatenate([zbuf[z, s, :, pl.ds(0, E)], zx[:, pl.ds(0, E)]], axis=0)
    text_id = jnp.where(mine_first < ROWS, (2 * z + s) * ROWS + mine_first, -1).astype(jnp.float32)
    ext_lane = lax.broadcasted_iota(jnp.int32, (2 * ROWS, EXT), 1)
    pos_pick = jnp.where(ext_lane == 0, 256.0, jnp.where(ext_lane == 1, 1.0, 0.0))
    pos_pick = pos_pick.astype(jnp.bfloat16)

    def embed(pooled):
        return unit_rows(dot_nn(pooled, projw_v[...])).astype(jnp.bfloat16)

    own_t[...] = jnp.zeros_like(own_t)

    def text_side(pooled, extras):
        audio = embed(pooled)
        logits = scale * dot_nt(own_texts, audio) + bias
        hit = dot_nt(pos_pick, extras) == text_id
        own_t[...] += dot_nn(weights_of(logits, hit), audio)

    def blocks_of(where):
        pooled = [pbuf[at_z(o)].reshape(2 * ROWS, CH) for o in where]
        extras = [zbuf[at_z(o), :, :, pl.ds(E, EXT)].reshape(2 * ROWS, EXT) for o in where]
        if len(where) == 1:
            return pooled[0], extras[0]
        return jnp.concatenate(pooled, axis=0), jnp.concatenate(extras, axis=0)

    def audio_side():
        audio_down.wait_recv()
        rows = jnp.concatenate([pbuf[z, s], px[...]], axis=0)
        audio = embed(rows)
        texts = zbuf[:, :, :, pl.ds(0, E)].reshape(nz * 2 * ROWS, E)
        logits = scale * dot_nt(audio, texts) + bias
        pos = jnp.concatenate([pos_col, jnp.full((ROWS, 1), -1, jnp.int32)], axis=0)
        hit = lax.broadcasted_iota(jnp.int32, logits.shape, 1) == pos
        own_a[...] = scale * dot_nn(weights_of(logits, hit), texts)
        back_a[...] = own_a[pl.ds(ROWS, ROWS), :].astype(jnp.bfloat16)
        return launch(remote(back_a, got_a, cross_send.at[2], cross_recv.at[2], {"grp": up}))

    lead = 2
    text_side(*blocks_of([0]))
    audio_up = None
    for d in range(1, far + 1):
        if d + lead <= far:
            relay(TEXT, d + lead)
        relay(AUDIO, d)
        text_side(*blocks_of([d, -d] if d < far else [d]))
        if d + lead == far + 1 or (audio_up is None and d == far):
            audio_up = audio_side()

    own_t[...] = scale * own_t[...]
    back_t[...] = own_t[pl.ds(ROWS, ROWS), :].astype(jnp.bfloat16)
    text_down = launch(remote(back_t, got_t, cross_send.at[3], cross_recv.at[3], {"grp": down}))

    audio_up.wait_recv()
    ag_ref[...] = own_a[pl.ds(0, ROWS), :] + got_a[...].astype(jnp.float32)
    text_down.wait_recv()
    tg_ref[...] = own_t[pl.ds(0, ROWS), :] + got_t[...].astype(jnp.float32)
    for copy in sent:
        copy.wait_send()


def on_device(nz, ng, clips, lengths, assign, text, positives, conv_w, proj_w, logit_scale, logit_bias):
    far = nz // 2
    smem = pl.BlockSpec(memory_space=pltpu.SMEM)
    vmem = pl.BlockSpec(memory_space=pltpu.VMEM)
    hbm = pl.BlockSpec(memory_space=pl.ANY)
    bf16, f32, dma = jnp.bfloat16, jnp.float32, pltpu.SemaphoreType.DMA
    out = jax.ShapeDtypeStruct((ROWS, E), f32)
    return pl.pallas_call(
        functools.partial(kernel, nz, ng),
        out_shape=(out, out),
        in_specs=[smem, smem, smem, vmem, vmem, hbm, hbm, hbm, hbm],
        out_specs=(vmem, vmem),
        scratch_shapes=[
            pltpu.VMEM((ROWS, E), bf16),
            pltpu.VMEM((ROWS, FRAMES, CH), bf16),
            pltpu.VMEM((3 * CH, CH), bf16),
            pltpu.VMEM((CH, E), bf16),
            pltpu.VMEM((CHUNK * HALF, 3 * CH), bf16),
            pltpu.VMEM((ROWS, CH), f32),
            pltpu.VMEM((nz, 2, ROWS, E + EXT), bf16),
            pltpu.VMEM((2, ROWS, CH), bf16),
            pltpu.VMEM((nz, 2, ROWS, CH), bf16),
            pltpu.VMEM((ROWS, E + EXT), bf16),
            pltpu.VMEM((ROWS, CH), bf16),
            pltpu.VMEM((2 * ROWS, E), f32),
            pltpu.VMEM((2 * ROWS, E), f32),
            pltpu.VMEM((ROWS, E), bf16),
            pltpu.VMEM((ROWS, E), bf16),
            pltpu.VMEM((ROWS, E), bf16),
            pltpu.VMEM((ROWS, E), bf16),
            dma((3 + ROWS // CHUNK,)),
            dma((2,)),
            dma((2,)),
            dma((2, 2, far, 2)),
            dma((2, 2, far, 2)),
            dma((4,)),
            dma((4,)),
        ],
        compiler_params=pltpu.CompilerParams(
            collective_id=0, has_side_effects=True, vmem_limit_bytes=67043328
        ),
        name="contrastive_step",
    )(
        logit_scale.reshape(1), logit_bias.reshape(1), lengths, assign, positives, text, clips,
        conv_w, proj_w,
    )


def solution(mesh):
    in_specs = (
        P(("grp", "blk", "sub"), None, None),
        P(("grp", "blk", "sub")),
        P(("grp", "blk"), "sub"),
        P(("grp", "blk", "sub"), None),
        P("grp", ("blk", "sub")),
        P(),
        P(),
        P(),
        P(),
    )
    out_specs = (P(("grp", "blk", "sub"), None), P(("grp", "blk", "sub"), None))
    body = functools.partial(on_device, mesh.shape["blk"], mesh.shape["grp"])
    return jax.shard_map(body, mesh=mesh, in_specs=in_specs, out_specs=out_specs, check_vma=False)
```

time: 189 us -> 66.8 us (0.35); the launches traced: 186 us -> 66.3 us
  waiting for transfers between devices: 63 us -> 0 us
  Pallas kernels: 0 us -> 61.4 us
  starting transfers between devices: 50.1 us -> 0 us
  local copies, waits for them, and re-layouts: 32.8 us -> 2.95 us
  between operations: 15.6 us -> 1.93 us
  matrix products: 10.9 us -> 0 us
  blocking collectives: 7.7 us -> 0 us
  other arithmetic: 6.2 us -> 0 us
    pallas_call x0 -> x1, Pallas kernels: none -> 61.4 us  [on_device(): pl.pallas_call(functools.partial(kernel, nz, ng), out_shape=(out, out), i...]
    all_gather x2 -> x0, waiting for transfers between devices: 37.4 us -> none  [gather_axes(): out = lax.all_gather(out, axes[number], axis=dim, tiled=True)]
    ppermute x2 -> x0, starting transfers between devices: 27.9 us -> none  [passed_along(): return lax.ppermute(block, axis, route)]
    slice x3 -> x0, local copies, waits for them, and re-layouts: 27.1 us -> none  [the longest x1 9.67 us: tower(): padded[:, 2:count_frames + 1:2]]
    all_to_all x3 -> x0, starting transfers between devices: 22.1 us -> none  [the longest x1 10 us: on_device(): lax.all_to_all(next_weights, ('blk', 'sub'), split_axis=1, concat_axis=0,...]
    all_to_all x3 -> x0, waiting for transfers between devices: 17.8 us -> none  [the longest x1 11.8 us: on_device(): lax.all_to_all(next_weights, ('blk', 'sub'), split_axis=1, concat_axis=0,...]
    dot_general x8 -> x0, matrix products: 10.9 us -> none  [the longest x2 2.49 us: left_product(): lax.dot_general(weights, block, (((0,), (0,)), ((), ())), preferred_eleme...]
    ppermute x2 -> x0, waiting for transfers between devices: 7.77 us -> none  [passed_along(): return lax.ppermute(block, axis, route)]
  transfers between devices with their start and end apart: 7 -> 0, of which waited for: 7 -> 0; matrix products, arithmetic and copies ran while one was open for 24% -> 0% of each run, Pallas kernels for 0% -> 0%
where the time goes in v1:
time: 66.8 us; the launch traced here: 66.3 us
  Pallas kernels  61.4 us (92%)
  local copies, waits for them, and re-layouts  2.95 us (4%)
  between operations  1.93 us (3%)
    pallas_call x1, Pallas kernels, on_device(): pl.pallas_call(functools.partial(kernel, nz, ng), out_shape=(out, out), i...  61.4 us
    unnamed x2, local copies, waits for them, and re-layouts  2.95 us

profile of v1, /device:TPU:1, one launch (start us, length us, event | category | flops | bytes accessed | tf_op | source)
XLA Modules:
  0.0 66.3 jit_solution(2183953072125541845)
XLA Ops:
  1.9 61.4 %contrastive_step.1 = (f32[16,1024]{1,0:T(8,128)}, f32[16,1024]{1,0:T(8,128)}) custom-call(f32[1]{0:T(128)} %bitcast.2.scale_ref, f32[1]{0:T(128)} %bitcast.3.bias_ref, s32[16]{0:T(128)} %len_ref.1, s32[1,16]{1,0:T(1,128)} %assign_ref.1, s32[1,16]{1,0:T(1,128)} %pos_ref.1, bf16[16,1024]{1,0:T(8,128)(2,1)} %text_hbm.1, bf16[16,128,512]{2,1,0:T(8,128)(2,1)} %clips_hbm.1, ...), custom_call_target="tpu_custom_call" | custom-call | tf_op jit(solution)/shard_map/contrastive_step/pallas_call | solution.py:281
  63.3 1.5 %copy.15 = f32[16,1024]{1,0:T(8,128)} copy(f32[16,1024]{1,0:T(8,128)} %get-tuple-element.4) | data formatting | bytes 131072
  64.8 1.5 %copy.16 = f32[16,1024]{1,0:T(8,128)} copy(f32[16,1024]{1,0:T(8,128)} %get-tuple-element.5) | data formatting | bytes 131072

commit v2 on v1

v2 whole, which is shorter than its diff:
```python
import functools
import math

import jax
import jax.numpy as jnp
from jax import lax
from jax.experimental import pallas as pl
from jax.experimental.pallas import tpu as pltpu
from jax.sharding import PartitionSpec as P

MESH = pl.DeviceIdType.MESH
ROWS = 16
FRAMES = 128
HALF = 64
CH = 512
E = 1024
EXT = 128
TEXT, AUDIO = 0, 1
TEXT_PARENT = {d: (d - 1) // 2 * 2 for d in range(1, 9)}
AUDIO_PARENT = {d: (d - 1) // 4 * 4 for d in range(1, 9)}
CHUNK = 4
EARLY = 2


def dot_nn(a, b):
    return jnp.dot(a, b, preferred_element_type=jnp.float32)


def dot_nt(a, b):
    return lax.dot_general(a, b, (((1,), (1,)), ((), ())), preferred_element_type=jnp.float32)


def gelu(x):
    inner = math.sqrt(2.0 / math.pi) * (x + 0.044715 * (x * x * x))
    return 0.5 * x * (1.0 + jnp.tanh(inner))


def unit_rows(wide):
    return wide * lax.rsqrt(jnp.sum(wide * wide, axis=1, keepdims=True) + 1e-06)


def weights_of(logits, hit):
    signed = jnp.where(hit, -logits, logits)
    s = jax.nn.sigmoid(signed)
    return jnp.where(hit, -s, s).astype(jnp.bfloat16)


def kernel(
    nz, ng,
    scale_ref, bias_ref, len_ref, assign_ref, pos_ref, text_hbm, clips_hbm, convw_hbm, projw_hbm,
    own_a, own_t, got_a, got_t,
    text_v, clips_v, convw_v, projw_v, picked, pool_f, zbuf, abuf, text_rows, pooled, slot_rows, info,
    part_a, part_t, back_a, back_t,
    load_sem, pair_send, pair_recv, ring_send, ring_recv, rows_send, rows_recv, part_send, part_recv,
):
    g, z, s = lax.axis_index("grp"), lax.axis_index("blk"), lax.axis_index("sub")
    other = 1 - s
    up, down = lax.rem(g + 1, ng), lax.rem(g + ng - 1, ng)
    far = nz // 2
    parents = {TEXT: TEXT_PARENT, AUDIO: AUDIO_PARENT}
    bufs = {TEXT: zbuf, AUDIO: abuf}
    scale, bias = scale_ref[0], bias_ref[0]
    sign1 = jnp.where(z < far, -1, 1)
    signs = (sign1, -sign1)

    def at_z(offset):
        return lax.rem(z + offset + 2 * nz, nz)

    n_chunks = ROWS // CHUNK
    loads = {"text": pltpu.make_async_copy(text_hbm, text_v, load_sem.at[0])}
    loads["conv"] = pltpu.make_async_copy(convw_hbm, convw_v, load_sem.at[1])
    loads["proj"] = pltpu.make_async_copy(projw_hbm, projw_v, load_sem.at[2])
    for i in range(n_chunks):
        part = pl.ds(i * CHUNK, CHUNK)
        loads[i] = pltpu.make_async_copy(clips_hbm.at[part], clips_v.at[part], load_sem.at[3 + i])
    for name in ("text", 0, "conv", *range(1, n_chunks), "proj"):
        loads[name].start()

    jumps = {d - p for table in parents.values() for d, p in table.items() if d <= far}
    barrier = pltpu.get_barrier_semaphore()
    greeted = [{"sub": other}]
    greeted += [{"grp": near_group, "sub": h} for near_group in (up, down) for h in (0, 1)]
    for place in sorted({j % nz for j in jumps} | {-j % nz for j in jumps}):
        greeted.append({"blk": at_z(place)})
    for device in greeted:
        pl.semaphore_signal(barrier, inc=1, device_id=device, device_id_type=MESH)

    sent = []

    def remote(src, dst, send, recv, device):
        return pltpu.make_async_remote_copy(
            src_ref=src, dst_ref=dst, send_sem=send, recv_sem=recv, device_id=device,
            device_id_type=MESH,
        )

    def launch(copy):
        copy.start()
        sent.append(copy)
        return copy

    def ring_copy(kind, sign, d, back):
        hop = d - parents[kind][d]
        here = bufs[kind].at[at_z(-sign * (d if back else d - hop))]
        way = (1 - sign) // 2
        return remote(
            here, here, ring_send.at[kind, way, d - 1], ring_recv.at[kind, way, d - 1],
            {"blk": at_z(sign * hop)},
        )

    def arrive(kind, sign, d):
        ring_copy(kind, sign, d, True).wait_recv()

    def pass_on(kind, sign, d):
        for child in range(far - 1, d, -1):
            if parents[kind][child] == d:
                launch(ring_copy(kind, sign, child, False))

    def pass_half_way(kind, d):
        if parents[kind][far] == d:
            launch(ring_copy(kind, -1, far, False))

    def set_out(kind):
        pass_half_way(kind, 0)
        for sign in signs:
            pass_on(kind, sign, 0)

    relays = {k: sorted({p for d, p in t.items() if d <= far and p > 0}) for k, t in parents.items()}
    leaves = {k: [d for d in range(1, far) if d not in relays[k]] for k in parents}

    def relay(kind):
        for d in relays[kind]:
            for sign in signs:
                arrive(kind, sign, d)
                pass_on(kind, sign, d)
            pass_half_way(kind, d)

    def leaf(kind, index):
        for d in leaves[kind]:
            arrive(kind, signs[index], d)

    def both_subs(src, dst, sems, group):
        for h in (0, 1):
            launch(
                remote(
                    src, dst, rows_send.at[sems, h], rows_recv.at[sems, s], {"grp": group, "sub": h}
                )
            )

    def both_came(dst, sems):
        for h in (0, 1):
            here = dst.at[2 + h]
            remote(
                here, here, rows_send.at[sems, h], rows_recv.at[sems, h], {"grp": up, "sub": h}
            ).wait_recv()

    def hand_back(src, dst, sems, group):
        launch(
            remote(src.at[other], dst.at[0], part_send.at[sems, 0], part_recv.at[sems, 0], {"sub": other})
        )
        for h in (0, 1):
            launch(
                remote(
                    src.at[2 + h], dst.at[1 + s], part_send.at[sems, 1 + h],
                    part_recv.at[sems, 1 + s], {"grp": group, "sub": h},
                )
            )

    def handed_back(dst, sems):
        for i in range(3):
            here = dst.at[i]
            remote(
                here, here, part_send.at[sems, i], part_recv.at[sems, i], {"sub": other}
            ).wait_recv()

    loads["text"].wait()
    zt = unit_rows(text_v[...].astype(jnp.float32)).astype(jnp.bfloat16)
    zbuf[z] = zt
    text_rows[s] = zt
    info[s, pl.ds(0, 1), pl.ds(0, ROWS)] = assign_ref[...]
    info[s, pl.ds(1, 1), pl.ds(0, ROWS)] = pos_ref[...]
    sub_id = lax.broadcasted_iota(jnp.int32, (ROWS, ROWS), 0)
    lane_id = lax.broadcasted_iota(jnp.int32, (ROWS, ROWS), 1)

    def column(row):
        return jnp.sum(jnp.where(sub_id == lane_id, row, 0), axis=1, keepdims=True)

    frame = lax.broadcasted_iota(jnp.int32, (3 * HALF, FRAMES), 1)
    place = lax.broadcasted_iota(jnp.int32, (3 * HALF, FRAMES), 0)
    tap = (place >= HALF).astype(jnp.int32) + (place >= 2 * HALF).astype(jnp.int32)
    wanted = 2 * (place - HALF * tap) + tap - 1
    out_id = lax.broadcasted_iota(jnp.int32, (HALF, CH), 0)

    def tower_chunk(i):
        loads[i].wait()
        for c in range(CHUNK):
            clip = i * CHUNK + c
            length = len_ref[clip]
            choose = jnp.where((wanted == frame) & (frame < length), 1.0, 0.0).astype(jnp.bfloat16)
            rows = dot_nn(choose, clips_v[clip]).astype(jnp.bfloat16)
            for k in range(3):
                picked[pl.ds(c * HALF, HALF), pl.ds(k * CH, CH)] = rows[k * HALF : (k + 1) * HALF]
        if i == 0:
            loads["conv"].wait()
        hidden = gelu(dot_nn(picked[...], convw_v[...]))
        for c in range(CHUNK):
            clip = i * CHUNK + c
            length = len_ref[clip]
            kept = jnp.where(2 * out_id < length, hidden[c * HALF : (c + 1) * HALF], 0.0)
            total = jnp.sum(kept, axis=0, keepdims=True)
            count = jnp.full((1, CH), (length + 1) >> 1, jnp.int32).astype(jnp.float32)
            pool_f[pl.ds(clip, 1), :] = total / count

    for i in range(EARLY):
        tower_chunk(i)
    pl.semaphore_wait(barrier, len(greeted))

    def to_partner(ref, index):
        return launch(
            remote(ref.at[s], ref.at[s], pair_send.at[index], pair_recv.at[index], {"sub": other})
        )

    def from_partner(ref, index):
        here = ref.at[other]
        remote(here, here, pair_send.at[index], pair_recv.at[index], {"sub": other}).wait_recv()

    to_partner(info, 0)
    set_out(TEXT)
    to_partner(text_rows, 1)
    both_subs(text_rows.at[s], text_rows.at[2 + s], 0, up)
    for i in range(EARLY, n_chunks):
        tower_chunk(i)

    from_partner(info, 0)
    clip_text = jnp.zeros((ROWS, 1), jnp.int32)
    for h in (0, 1):
        fills = info[h, pl.ds(0, 1), pl.ds(0, ROWS)] == sub_id + s * ROWS
        texts = jnp.where(fills, info[h, pl.ds(1, 1), pl.ds(0, ROWS)], 0)
        clip_text += jnp.sum(texts, axis=1, keepdims=True)
    lane = lax.broadcasted_iota(jnp.int32, (ROWS, EXT), 1)
    extra = jnp.where(lane == 0, clip_text >> 8, jnp.where(lane == 1, clip_text & 255, 0))
    own_pooled = pool_f[...].astype(jnp.bfloat16)
    pooled[s] = own_pooled
    abuf[z, :, pl.ds(0, CH)] = own_pooled
    abuf[z, :, pl.ds(CH, EXT)] = extra.astype(jnp.float32).astype(jnp.bfloat16)
    to_partner(pooled, 2)
    set_out(AUDIO)

    relay(TEXT)

    loads["proj"].wait()
    from_partner(pooled, 2)
    pair_assign = [column(info[h, pl.ds(0, 1), pl.ds(0, ROWS)]) for h in (0, 1)]
    pair_pos = [column(info[h, pl.ds(1, 1), pl.ds(0, ROWS)]) for h in (0, 1)]
    clip_id = lax.broadcasted_iota(jnp.int32, (2 * ROWS, 2 * ROWS), 1)
    order = jnp.where(jnp.concatenate(pair_assign, axis=0) == clip_id, 1.0, 0.0)
    slots = dot_nn(order.astype(jnp.bfloat16), pooled[...].reshape(2 * ROWS, CH))
    slot_rows[pl.ds(0, 2)] = slots.astype(jnp.bfloat16).reshape(2, ROWS, CH)
    both_subs(slot_rows.at[s], slot_rows.at[2 + s], 1, down)

    relay(AUDIO)

    def embed(rows):
        return unit_rows(dot_nn(rows, projw_v[...])).astype(jnp.bfloat16)

    leaf(TEXT, 0)
    leaf(TEXT, 1)
    arrive(TEXT, -1, far)
    both_came(slot_rows, 1)
    audio = embed(slot_rows[...].reshape(4 * ROWS, CH))
    texts = zbuf[...].reshape(nz * ROWS, E)
    logits = scale * dot_nt(audio, texts) + bias
    pos = jnp.concatenate([*pair_pos, jnp.full((2 * ROWS, 1), -1, jnp.int32)], axis=0)
    text_at = lax.broadcasted_iota(jnp.int32, logits.shape, 1)
    hit = 2 * text_at - (text_at & (ROWS - 1)) + ROWS * s == pos
    grad_a = scale * dot_nn(weights_of(logits, hit), texts)
    part_a[...] = grad_a.reshape(4, ROWS, E)
    back_a[...] = grad_a.astype(jnp.bfloat16).reshape(4, ROWS, E)
    hand_back(back_a, got_a, 0, up)
    own_a[...] = part_a[s]

    from_partner(text_rows, 1)
    both_came(text_rows, 0)
    row = lax.broadcasted_iota(jnp.int32, (4 * ROWS, 1), 0)
    own_texts = text_rows[...].reshape(4 * ROWS, E)
    text_id = jnp.where(row < 2 * ROWS, 2 * ROWS * z + row, -1).astype(jnp.float32)
    ext_lane = lax.broadcasted_iota(jnp.int32, (4 * ROWS, EXT), 1)
    pos_pick = jnp.where(ext_lane == 0, 256.0, jnp.where(ext_lane == 1, 1.0, 0.0))
    pos_pick = pos_pick.astype(jnp.bfloat16)

    def text_side(offsets):
        rows = jnp.concatenate([abuf[at_z(o)] for o in offsets], axis=0)
        audio = embed(rows[:, :CH])
        logits = scale * dot_nt(own_texts, audio) + bias
        hit = dot_nt(pos_pick, rows[:, CH:]) == text_id
        return dot_nn(weights_of(logits, hit), audio)

    leaf(AUDIO, 0)
    part_t[...] = text_side([-sign1 * d for d in range(far)]).reshape(4, ROWS, E)
    leaf(AUDIO, 1)
    arrive(AUDIO, -1, far)
    rest = text_side([sign1 * d for d in range(1, far + 1)]).reshape(4, ROWS, E)
    total = scale * (part_t[...] + rest)
    part_t[...] = total
    back_t[...] = total.astype(jnp.bfloat16)
    hand_back(back_t, got_t, 1, down)
    own_t[...] = part_t[s]

    handed_back(got_a, 0)
    handed_back(got_t, 1)
    for copy in sent:
        copy.wait_send()


def add_up(own_a, own_t, got_a, got_t, ag_ref, tg_ref):
    ag_ref[...] = own_a[...] + jnp.sum(got_a[...].astype(jnp.float32), axis=0)
    tg_ref[...] = own_t[...] + jnp.sum(got_t[...].astype(jnp.float32), axis=0)


def on_device(nz, ng, clips, lengths, assign, text, positives, conv_w, proj_w, logit_scale, logit_bias):
    far = nz // 2
    smem = pl.BlockSpec(memory_space=pltpu.SMEM)
    vmem = pl.BlockSpec(memory_space=pltpu.VMEM)
    hbm = pl.BlockSpec(memory_space=pl.ANY)
    bf16, f32, dma = jnp.bfloat16, jnp.float32, pltpu.SemaphoreType.DMA
    wide = jax.ShapeDtypeStruct((ROWS, E), f32)
    short = jax.ShapeDtypeStruct((3, ROWS, E), bf16)
    parts = pl.pallas_call(
        functools.partial(kernel, nz, ng),
        out_shape=(wide, wide, short, short),
        in_specs=[smem, smem, smem, vmem, vmem, hbm, hbm, hbm, hbm],
        out_specs=(vmem, vmem, vmem, vmem),
        scratch_shapes=[
            pltpu.VMEM((ROWS, E), bf16),
            pltpu.VMEM((ROWS, FRAMES, CH), bf16),
            pltpu.VMEM((3 * CH, CH), bf16),
            pltpu.VMEM((CH, E), bf16),
            pltpu.VMEM((CHUNK * HALF, 3 * CH), bf16),
            pltpu.VMEM((ROWS, CH), f32),
            pltpu.VMEM((nz, ROWS, E), bf16),
            pltpu.VMEM((nz, ROWS, CH + EXT), bf16),
            pltpu.VMEM((4, ROWS, E), bf16),
            pltpu.VMEM((2, ROWS, CH), bf16),
            pltpu.VMEM((4, ROWS, CH), bf16),
            pltpu.VMEM((2, 8, 128), jnp.int32),
            pltpu.VMEM((4, ROWS, E), f32),
            pltpu.VMEM((4, ROWS, E), f32),
            pltpu.VMEM((4, ROWS, E), bf16),
            pltpu.VMEM((4, ROWS, E), bf16),
            dma((3 + ROWS // CHUNK,)),
            dma((3,)),
            dma((3,)),
            dma((2, 2, far)),
            dma((2, 2, far)),
            dma((2, 2)),
            dma((2, 2)),
            dma((2, 3)),
            dma((2, 3)),
        ],
        compiler_params=pltpu.CompilerParams(
            collective_id=0, has_side_effects=True, vmem_limit_bytes=67043328
        ),
        name="contrastive_step",
    )(
        logit_scale.reshape(1), logit_bias.reshape(1), lengths, assign, positives, text, clips,
        conv_w, proj_w,
    )
    return pl.pallas_call(
        add_up,
        out_shape=(wide, wide),
        in_specs=[vmem] * 4,
        out_specs=(vmem, vmem),
        name="add_up",
    )(*parts)


def solution(mesh):
    in_specs = (
        P(("grp", "blk", "sub"), None, None),
        P(("grp", "blk", "sub")),
        P(("grp", "blk"), "sub"),
        P(("grp", "blk", "sub"), None),
        P("grp", ("blk", "sub")),
        P(),
        P(),
        P(),
        P(),
    )
    out_specs = (P(("grp", "blk", "sub"), None), P(("grp", "blk", "sub"), None))
    body = functools.partial(on_device, mesh.shape["blk"], mesh.shape["grp"])
    return jax.shard_map(body, mesh=mesh, in_specs=in_specs, out_specs=out_specs, check_vma=False)
```

time: 66.8 us -> 53.6 us (0.80)
  Pallas kernels: 61.4 us -> 51.4 us
  local copies, waits for them, and re-layouts: 2.95 us -> 0 us
    pallas_call x1 -> x2, Pallas kernels: 61.4 us -> 51.4 us  [the longest x1 49.7 us: on_device(): pl.pallas_call(functools.partial(kernel, nz, ng), out_shape=(wide, wide,...]
    unnamed x2 -> x0, local copies, waits for them, and re-layouts: 2.95 us -> none
where the time goes in v2:
time: 53.6 us; the launch traced here: 53.4 us
  Pallas kernels  51.4 us (96%)
  between operations  1.93 us (4%)
    pallas_call x1, Pallas kernels, on_device(): pl.pallas_call(functools.partial(kernel, nz, ng), out_shape=(wide, wide,...  49.7 us
    pallas_call x1, Pallas kernels, on_device(): pl.pallas_call(add_up, out_shape=(wide, wide), in_specs=[vmem] * 4, out_s...  1.68 us

profile of v2, /device:TPU:1, one launch (start us, length us, event | category | flops | bytes accessed | tf_op | source)
XLA Modules:
  0.0 53.4 jit_solution(12809807778627863860)
XLA Ops:
  1.9 49.7 %contrastive_step.1 = (f32[16,1024]{1,0:T(8,128)}, f32[16,1024]{1,0:T(8,128)}, bf16[3,16,1024]{2,1,0:T(8,128)(2,1)}, bf16[3,16,1024]{2,1,0:T(8,128)(2,1)}) custom-call(f32[1]{0:T(128)} %bitcast.2.scale_ref, f32[1]{0:T(128)} %bitcast.3.bias_ref, s32[16]{0:T(128)} %len_ref.1, s32[1,16]{1,0:T(1,128)} %assign_ref.1, s32[1,16]{1,0:T(1,128)} %pos_ref.1, ...), custom_call_target="tpu_custom_call" | custom-call | tf_op jit(solution)/shard_map/contrastive_step/pallas_call | solution.py:327
  51.7 1.7 %add_up.1 = (f32[16,1024]{1,0:T(8,128)}, f32[16,1024]{1,0:T(8,128)}) custom-call(f32[16,1024]{1,0:T(8,128)} %get-tuple-element.6.own_a, f32[16,1024]{1,0:T(8,128)} %get-tuple-element.7.own_t, bf16[3,16,1024]{2,1,0:T(8,128)(2,1)} %get-tuple-element.8.got_a, bf16[3,16,1024]{2,1,0:T(8,128)(2,1)} %get-tuple-element.9.got_t), custom_call_target="tpu_custom_call" | custom-call | tf_op jit(solution)/shard_map/add_up/pallas_call | solution.py:367

commit v3 on v2

--- a/solution.py
+++ b/solution.py
@@ -16,10 +16,9 @@
 E = 1024
 EXT = 128
 TEXT, AUDIO = 0, 1
-TEXT_PARENT = {d: (d - 1) // 2 * 2 for d in range(1, 9)}
-AUDIO_PARENT = {d: (d - 1) // 4 * 4 for d in range(1, 9)}
+TEXT_PARENT = {1: 0, 2: 1, 3: 0, 4: 3, 5: 4, 6: 3, 7: 6, 8: 6}
+AUDIO_PARENT = {1: 0, 2: 0, 3: 2, 4: 2, 5: 0, 6: 5, 7: 5, 8: 5}
 CHUNK = 4
-EARLY = 2
 
 
 def dot_nn(a, b):
@@ -154,9 +153,6 @@
             ).wait_recv()
 
     def hand_back(src, dst, sems, group):
-        launch(
-            remote(src.at[other], dst.at[0], part_send.at[sems, 0], part_recv.at[sems, 0], {"sub": other})
-        )
         for h in (0, 1):
             launch(
                 remote(
@@ -164,6 +160,9 @@
                     part_recv.at[sems, 1 + s], {"grp": group, "sub": h},
                 )
             )
+        launch(
+            remote(src.at[other], dst.at[0], part_send.at[sems, 0], part_recv.at[sems, 0], {"sub": other})
+        )
 
     def handed_back(dst, sems):
         for i in range(3):
@@ -190,8 +189,9 @@
     wanted = 2 * (place - HALF * tap) + tap - 1
     out_id = lax.broadcasted_iota(jnp.int32, (HALF, CH), 0)
 
-    def tower_chunk(i):
-        loads[i].wait()
+    def tower_chunk(i, carry):
+        part = pl.ds(i * CHUNK, CHUNK)
+        pltpu.make_async_copy(clips_hbm.at[part], clips_v.at[part], load_sem.at[3 + i]).wait()
         for c in range(CHUNK):
             clip = i * CHUNK + c
             length = len_ref[clip]
@@ -199,8 +199,6 @@
             rows = dot_nn(choose, clips_v[clip]).astype(jnp.bfloat16)
             for k in range(3):
                 picked[pl.ds(c * HALF, HALF), pl.ds(k * CH, CH)] = rows[k * HALF : (k + 1) * HALF]
-        if i == 0:
-            loads["conv"].wait()
         hidden = gelu(dot_nn(picked[...], convw_v[...]))
         for c in range(CHUNK):
             clip = i * CHUNK + c
@@ -209,9 +207,11 @@
             total = jnp.sum(kept, axis=0, keepdims=True)
             count = jnp.full((1, CH), (length + 1) >> 1, jnp.int32).astype(jnp.float32)
             pool_f[pl.ds(clip, 1), :] = total / count
-
-    for i in range(EARLY):
-        tower_chunk(i)
+        return carry
+
+    early = jnp.clip((nz - 1 - z) * 4 // CHUNK, 1, n_chunks)
+    loads["conv"].wait()
+    lax.fori_loop(0, early, tower_chunk, 0)
     pl.semaphore_wait(barrier, len(greeted))
 
     def to_partner(ref, index):
@@ -227,8 +227,7 @@
     set_out(TEXT)
     to_partner(text_rows, 1)
     both_subs(text_rows.at[s], text_rows.at[2 + s], 0, up)
-    for i in range(EARLY, n_chunks):
-        tower_chunk(i)
+    lax.fori_loop(early, n_chunks, tower_chunk, 0)
 
     from_partner(info, 0)
     clip_text = jnp.zeros((ROWS, 1), jnp.int32)

time: 53.6 us -> 52.1 us (0.972)
  Pallas kernels: 51.4 us -> 49.9 us
    pallas_call x1, Pallas kernels: 49.7 us -> 48.3 us  [on_device(): pl.pallas_call(functools.partial(kernel, nz, ng), out_shape=(wide, wide,...]
where the time goes in v3:
time: 52.1 us; the launch traced here: 51.9 us
  Pallas kernels  49.9 us (96%)
  between operations  1.93 us (4%)
    pallas_call x1, Pallas kernels, on_device(): pl.pallas_call(functools.partial(kernel, nz, ng), out_shape=(wide, wide,...  48.3 us
    pallas_call x1, Pallas kernels, on_device(): pl.pallas_call(add_up, out_shape=(wide, wide), in_specs=[vmem] * 4, out_s...  1.68 us

profile of v3, /device:TPU:1, one launch (start us, length us, event | category | flops | bytes accessed | tf_op | source)
XLA Modules:
  0.0 51.9 jit_solution(10210714445568328783)
XLA Ops:
  1.9 48.3 %contrastive_step.1 = (f32[16,1024]{1,0:T(8,128)}, f32[16,1024]{1,0:T(8,128)}, bf16[3,16,1024]{2,1,0:T(8,128)(2,1)}, bf16[3,16,1024]{2,1,0:T(8,128)(2,1)}) custom-call(f32[1]{0:T(128)} %bitcast.2.scale_ref, f32[1]{0:T(128)} %bitcast.3.bias_ref, s32[16]{0:T(128)} %len_ref.1, s32[1,16]{1,0:T(1,128)} %assign_ref.1, s32[1,16]{1,0:T(1,128)} %pos_ref.1, ...), custom_call_target="tpu_custom_call" | custom-call | tf_op jit(solution)/shard_map/contrastive_step/pallas_call | solution.py:326
  50.2 1.7 %add_up.1 = (f32[16,1024]{1,0:T(8,128)}, f32[16,1024]{1,0:T(8,128)}) custom-call(f32[16,1024]{1,0:T(8,128)} %get-tuple-element.6.own_a, f32[16,1024]{1,0:T(8,128)} %get-tuple-element.7.own_t, bf16[3,16,1024]{2,1,0:T(8,128)(2,1)} %get-tuple-element.8.got_a, bf16[3,16,1024]{2,1,0:T(8,128)(2,1)} %get-tuple-element.9.got_t), custom_call_target="tpu_custom_call" | custom-call | tf_op jit(solution)/shard_map/add_up/pallas_call | solution.py:366

commit v4 on v3

--- a/solution.py
+++ b/solution.py
@@ -18,6 +18,7 @@
 TEXT, AUDIO = 0, 1
 TEXT_PARENT = {1: 0, 2: 1, 3: 0, 4: 3, 5: 4, 6: 3, 7: 6, 8: 6}
 AUDIO_PARENT = {1: 0, 2: 0, 3: 2, 4: 2, 5: 0, 6: 5, 7: 5, 8: 5}
+HALF_WAY = {TEXT: 1, AUDIO: -1}
 CHUNK = 4
 
 
@@ -116,7 +117,7 @@
 
     def pass_half_way(kind, d):
         if parents[kind][far] == d:
-            launch(ring_copy(kind, -1, far, False))
+            launch(ring_copy(kind, HALF_WAY[kind], far, False))
 
     def set_out(kind):
         pass_half_way(kind, 0)
@@ -263,7 +264,7 @@
 
     leaf(TEXT, 0)
     leaf(TEXT, 1)
-    arrive(TEXT, -1, far)
+    arrive(TEXT, HALF_WAY[TEXT], far)
     both_came(slot_rows, 1)
     audio = embed(slot_rows[...].reshape(4 * ROWS, CH))
     texts = zbuf[...].reshape(nz * ROWS, E)
@@ -296,7 +297,7 @@
     leaf(AUDIO, 0)
     part_t[...] = text_side([-sign1 * d for d in range(far)]).reshape(4, ROWS, E)
     leaf(AUDIO, 1)
-    arrive(AUDIO, -1, far)
+    arrive(AUDIO, HALF_WAY[AUDIO], far)
     rest = text_side([sign1 * d for d in range(1, far + 1)]).reshape(4, ROWS, E)
     total = scale * (part_t[...] + rest)
     part_t[...] = total

time: 52.1 us -> 52.9 us (1.015)
  Pallas kernels: 49.9 us -> 50.8 us
    pallas_call x1, Pallas kernels: 48.3 us -> 49.1 us  [on_device(): pl.pallas_call(functools.partial(kernel, nz, ng), out_shape=(wide, wide,...]
where the time goes in v4:
time: 52.9 us; the launch traced here: 52.7 us
  Pallas kernels  50.8 us (96%)
  between operations  1.93 us (4%)
    pallas_call x1, Pallas kernels, on_device(): pl.pallas_call(functools.partial(kernel, nz, ng), out_shape=(wide, wide,...  49.1 us
    pallas_call x1, Pallas kernels, on_device(): pl.pallas_call(add_up, out_shape=(wide, wide), in_specs=[vmem] * 4, out_s...  1.68 us

profile of v4, /device:TPU:1, one launch (start us, length us, event | category | flops | bytes accessed | tf_op | source)
XLA Modules:
  0.0 52.7 jit_solution(9975764519994807571)
XLA Ops:
  1.9 49.1 %contrastive_step.1 = (f32[16,1024]{1,0:T(8,128)}, f32[16,1024]{1,0:T(8,128)}, bf16[3,16,1024]{2,1,0:T(8,128)(2,1)}, bf16[3,16,1024]{2,1,0:T(8,128)(2,1)}) custom-call(f32[1]{0:T(128)} %bitcast.2.scale_ref, f32[1]{0:T(128)} %bitcast.3.bias_ref, s32[16]{0:T(128)} %len_ref.1, s32[1,16]{1,0:T(1,128)} %assign_ref.1, s32[1,16]{1,0:T(1,128)} %pos_ref.1, ...), custom_call_target="tpu_custom_call" | custom-call | tf_op jit(solution)/shard_map/contrastive_step/pallas_call | solution.py:327
  51.0 1.7 %add_up.1 = (f32[16,1024]{1,0:T(8,128)}, f32[16,1024]{1,0:T(8,128)}) custom-call(f32[16,1024]{1,0:T(8,128)} %get-tuple-element.6.own_a, f32[16,1024]{1,0:T(8,128)} %get-tuple-element.7.own_t, bf16[3,16,1024]{2,1,0:T(8,128)(2,1)} %get-tuple-element.8.got_a, bf16[3,16,1024]{2,1,0:T(8,128)(2,1)} %get-tuple-element.9.got_t), custom_call_target="tpu_custom_call" | custom-call | tf_op jit(solution)/shard_map/add_up/pallas_call | solution.py:367
